TPU v7x, 128 devices: a whole 4x4x4 slice. The times are simulated.
128 devices in a mesh: tm: 4 (over x_hi, core), slope: 32 (over x_lo, z, y).
Axes of the slice: x: 4 (x_hi: 2, x_lo: 2; x = x_hi * 2 + x_lo), y: 4, z: 4, core: 2. Of those that a mesh axis runs over, the one named last changes fastest.
Arguments:
- telemetry: bfloat16 [32, 32, 96, 4096], P('slope', None, None, 'tm'), may hold values from -24 to 24
- frame_ids: int32 [4096], P('tm'), may hold values from 0 to 1023, as said below
- valid: int32 [8, 48], replicated, may hold values 0 or 1
- noise: float32 [1024], replicated, may hold values from 0.1 to 1
- prior_next: float32 [32, 32, 96, 1024], P('slope', 'tm'), may hold values from -2 to 2
Outputs:
- panel: float32 [32, 32, 96, 1024], P('slope', 'tm')
- next_block: float32 [32, 32, 96, 1024], P('slope', 'tm')
Inputs may be any that keep to these rules, and one draw needn't show every extreme that they name: `frame_ids`: entry f names a frame of the block of 1024 buffer frames that starts at (f // 1024) * 1024; entries may repeat.
All inputs are finite; a program needn't handle non-finite values.
Results may differ from a plain program's by a relative error of at most 0.0003.
Values may be sent and summed in bfloat16 or wider, within the bound.
No kernel may reach another device: no remote copies, remote signals or barrier semaphores. Data moves between devices by JAX's collectives and lax.ppermute only.
A program may use at most 128 MiB of HBM per device.

v0:
```python
import jax
import jax.numpy as jnp
from jax import lax
from jax.experimental import pallas as pl
from jax.experimental.pallas import tpu as pltpu
from jax.sharding import PartitionSpec as P

NB = 128
MB = 8
TN = (((0,), (0,)), ((), ()))
NT = (((1,), (1,)), ((), ()))
WHOLE = pl.BlockSpec(memory_space=pltpu.VMEM)


def in_hbm(value):
    return pltpu.with_memory_space_constraint(value, pltpu.HBM)


def params(mib=40):
    return pltpu.CompilerParams(vmem_limit_bytes=mib * 2**20)


def bf16_round(z):
    return z.astype(jnp.bfloat16).astype(jnp.float32)


def split3(z):
    high = bf16_round(z)
    rest = z - high
    mid = bf16_round(rest)
    return high, mid, rest - mid


def row_of(z, j):
    return jnp.broadcast_to(z[j:j + 1, :], z.shape)


AHEAD = 2


def factor_block(wa, wx, out):
    sub = lax.broadcasted_iota(jnp.int32, (MB, NB), 0)
    groups = NB // MB
    rows_of = lambda k: (wa[k * MB:(k + 1) * MB, :], wx[k * MB:(k + 1) * MB, :])
    window = [rows_of(k) for k in range(AHEAD)]
    for k in range(groups):
        lo = MB * k
        if k + AHEAD < groups:
            window.append(rows_of(k + AHEAD))
        a, x = window.pop(0)
        columns = lambda z: [jnp.broadcast_to(z[:, lo + j:lo + j + 1], (MB, NB)) for j in range(MB)]
        cols = columns(a)
        others = [[na, nx, columns(na)] for na, nx in window]
        inv_d = jnp.zeros((MB, NB), jnp.float32)
        piv = jnp.zeros((MB, NB), jnp.float32)
        for j in range(MB):
            pivot = row_of(cols[j], j)
            recip = 1.0 / pivot
            mult = jnp.where(sub > j, cols[j] * recip, 0.0)
            ra, rx = row_of(a, j), row_of(x, j)
            rcs = {l: row_of(cols[l], j) for l in range(j + 1, MB)}
            for other in others:
                nmult = other[2][j] * recip
                other[0] = other[0] - nmult * ra
                other[1] = other[1] - nmult * rx
                for l in range(j + 1, MB):
                    other[2][l] = other[2][l] - nmult * rcs[l]
            for l in range(j + 1, MB):
                cols[l] = cols[l] - mult * rcs[l]
            a = a - mult * ra
            x = x - mult * rx
            inv_d = jnp.where(sub == j, recip, inv_d)
            piv = jnp.where(sub == j, pivot, piv)
        window = [(other[0], other[1]) for other in others]
        out[lo:lo + MB, :] = x * (1.0 / jnp.sqrt(piv))
        top = lo + (1 + AHEAD) * MB
        if top < NB:
            right = jnp.concatenate([a * inv_d, x * inv_d], axis=1)
            lh, lm, ll = split3(a)
            rh, rm, rl = split3(right)
            left_stack = jnp.concatenate([lh, lh, lm, lh, ll, lm], axis=0).astype(jnp.bfloat16)
            right_stack = jnp.concatenate([rh, rm, rh, rl, rh, rm], axis=0).astype(jnp.bfloat16)
            prod = lax.dot_general(left_stack, right_stack, TN, preferred_element_type=jnp.float32)
            wa[top:, :] = wa[top:, :] - prod[top:, :NB]
            wx[top:, :] = wx[top:, :] - prod[top:, NB:]


def chol_panels(first, count, src, dst, big, wa, wx, linv, ys, arrive, leave):
    n = big.shape[0]
    nblk = n // NB
    last = first + count - 1
    rows = lax.broadcasted_iota(jnp.int32, (NB, NB), 0)
    lanes = lax.broadcasted_iota(jnp.int32, (NB, NB), 1)
    eye = jnp.where(rows == lanes, 1.0, 0.0)

    def block(i):
        return pl.ds(pl.multiple_of(i * NB, NB), NB)

    def load(i):
        return pltpu.make_async_copy(src.at[block(i)], big.at[block(i)], arrive.at[i])

    def store(i):
        return pltpu.make_async_copy(big.at[block(i)], dst.at[block(i)], leave.at[i])

    for i in range(first, nblk):
        load(i).start()
    load(first).wait()

    def panel_step(p, carry):
        at = pl.multiple_of(p * NB, NB)
        wa[...] = big[pl.ds(at, NB), pl.ds(at, NB)]
        wx[...] = eye
        big[pl.ds(at, NB), pl.ds(at, NB)] = eye
        factor_block(wa, wx, linv)
        ih, im, il = (part.astype(jnp.bfloat16) for part in split3(linv[...]))
        rh, rm, rl = (part.astype(jnp.bfloat16) for part in split3(big[pl.ds(at, NB), :]))
        mul = lambda u, v: jnp.dot(jnp.concatenate(u, axis=1), jnp.concatenate(v, axis=0), preferred_element_type=jnp.float32)
        y = mul((ih, im), (rh, rm)) + (mul((im, ih), (rh, rm)) + mul((il, ih), (rh, rl)))
        big[pl.ds(at, NB), :] = y
        store(p).start()
        high, mid, low = (part.astype(jnp.bfloat16) for part in split3(y))
        for i, part in enumerate((high, mid, low, high)):
            ys[i * NB:(i + 1) * NB, :] = part

        def trail(u, c):
            row = pl.multiple_of(u * 2 * NB, 2 * NB)
            wide = pl.ds(row, 2 * NB)
            hm = ys[0:2 * NB, wide]
            mh = jnp.concatenate([ys[NB:2 * NB, wide], ys[0:NB, wide]], axis=0)
            lh = ys[2 * NB:4 * NB, wide]
            hl = jnp.concatenate([ys[0:NB, :], ys[2 * NB:3 * NB, :]], axis=0)
            dot = lambda u, v: lax.dot_general(u, v, TN, preferred_element_type=jnp.float32)
            upd = dot(hm, ys[0:2 * NB, :]) + (dot(mh, ys[0:2 * NB, :]) + dot(lh, hl))
            for h in range(2):
                i = 2 * u + h

                @pl.when(jnp.logical_and(i > p, p == first))
                def _():
                    load(i).wait()

                @pl.when(i > p)
                def _():
                    big[block(i), pl.ds(at, NB)] = jnp.zeros((NB, NB), jnp.float32)
                    big[block(i), :] = big[block(i), :] - upd[h * NB:(h + 1) * NB]

                @pl.when(jnp.logical_and(i > p, p == last))
                def _():
                    store(i).start()
            return c

        lax.fori_loop((p + 1) // 2, nblk // 2, trail, 0)
        return carry

    lax.fori_loop(first, last + 1, panel_step, 0)
    for i in range(first, nblk):
        store(i).wait()


CHOL_SCRATCH = [pltpu.VMEM((NB, NB), jnp.float32)] * 3


def chol_step(src, first, count):
    n = src.shape[0]
    blocks = n // NB

    def kernel(src_ref, dst_ref, big, wa, wx, linv, ys, arrive, leave):
        chol_panels(first, count, src_ref, dst_ref, big, wa, wx, linv, ys, arrive, leave)

    hbm = pl.BlockSpec(memory_space=pltpu.HBM)
    return pl.pallas_call(
        kernel, out_shape=pltpu.HBM((n, n), jnp.float32), in_specs=[hbm], out_specs=hbm,
        scratch_shapes=[pltpu.VMEM((n, n), jnp.float32)] + CHOL_SCRATCH
        + [pltpu.VMEM((4 * NB, n), jnp.bfloat16), pltpu.SemaphoreType.DMA((blocks,)), pltpu.SemaphoreType.DMA((blocks,))],
        input_output_aliases={0: 0}, compiler_params=params(24), name="chol_panels")(in_hbm(src))


SPLIT = (2, 5, 1)
AXES = ("tm", "slope")
RING = 4
SCALARS = pl.BlockSpec(memory_space=pltpu.SMEM)
HBM = pl.BlockSpec(memory_space=pltpu.HBM)


def pick_first(tel, ids, valid, place):
    rows, _, frames = tel.shape
    half = rows // 2

    def kernel(place_ref, tel_hbm, ids_ref, valid_ref, mine_ref, theirs_ref, second_ref, hot_ref, got, lead, tel_ref, sem):
        fetch = pltpu.make_async_copy(tel_hbm.at[:, pl.ds(0, 16), :], tel_ref, sem)
        fetch.start()
        hot_ref[...] = jnp.where(lax.broadcasted_iota(jnp.int32, (frames, frames), 0) == ids_ref[...], 1.0, 0.0).astype(jnp.bfloat16)
        fetch.wait()
        got[...] = tel_ref[...].astype(jnp.float32)
        both = jnp.concatenate([got[:, 0, :], got[:, 1, :]], axis=0).astype(jnp.bfloat16)
        both = jnp.dot(both, hot_ref[...], preferred_element_type=jnp.float32)
        kept = [valid_ref[0, 4 * c + place_ref[1]].astype(jnp.float32) for c in range(2)]
        lead[...] = both[:rows] * kept[0]
        at = pl.multiple_of(place_ref[0] * half, half)
        mine_ref[...] = lead[pl.ds(at, half), :].astype(jnp.bfloat16)
        theirs_ref[...] = lead[pl.ds(pl.multiple_of(half - at, half), half), :].astype(jnp.bfloat16)
        second_ref[...] = (both[rows:] * kept[1]).astype(jnp.bfloat16)

    whole = lambda shape: pl.BlockSpec(shape, lambda i: (0,) * len(shape))
    shapes = ((half, frames), (half, frames), (rows, frames), (frames, frames))
    return pl.pallas_call(
        kernel,
        grid=(1,),
        out_shape=tuple(jax.ShapeDtypeStruct(s, jnp.bfloat16) for s in shapes),
        in_specs=[SCALARS, HBM, whole((1, frames)), SCALARS],
        out_specs=tuple(whole(s) for s in shapes),
        scratch_shapes=[pltpu.VMEM((rows, 16, frames), jnp.float32), pltpu.VMEM((rows, frames), jnp.float32),
                        pltpu.VMEM((rows, 16, frames), tel.dtype), pltpu.SemaphoreType.DMA],
        compiler_params=params(), name="pick_first")(place, in_hbm(tel), ids, valid)


def pick_all(tel, hot, keep, tm_index):
    rows, cycles, frames = tel.shape
    per = 4
    quarter = rows // RING
    steps = quarter // per

    def kernel(tm_ref, tel_ref, hot_ref, keep_ref, *outs):
        got = jnp.dot(tel_ref[...].reshape(per * cycles, frames), hot_ref[...], preferred_element_type=jnp.float32)
        got = (got.reshape(per, cycles, frames) * keep_ref[...][None]).astype(jnp.bfloat16)
        for k in range(RING):
            @pl.when(pl.program_id(0) // steps == k)
            def _():
                outs[k][...] = got

    place = lambda k: pl.BlockSpec((per, cycles, frames), lambda i, tm: (jnp.clip(i - steps * k, 0, steps - 1), 0, 0))
    return pl.pallas_call(
        kernel, out_shape=(pltpu.HBM((quarter, cycles, frames), jnp.bfloat16),) * RING,
        grid_spec=pltpu.PrefetchScalarGridSpec(
            num_scalar_prefetch=1, grid=(rows // per,),
            in_specs=[pl.BlockSpec((per, cycles, frames), lambda i, tm: (jnp.bitwise_xor(tm[0], i // steps) * steps + i % steps, 0, 0)),
                      pl.BlockSpec((frames, frames), lambda i, tm: (0, 0)), pl.BlockSpec(keep.shape, lambda i, tm: (0, 0))],
            out_specs=tuple(place(k) for k in range(RING))),
        compiler_params=params(), name="pick_all")(tm_index, in_hbm(tel), hot, keep)


def lead_gram(own, other, second_rows, noise, place):
    width = noise.shape[1]
    tm_count, quarter, frames = second_rows.shape
    half = own[0].shape[3]
    scale = 1.0 / (tm_count * frames)
    group = 2 * RING
    extra = 16

    def kernel(place_ref, *refs):
        parts = (refs[:RING], refs[RING:2 * RING])
        rows_ref, noise_ref, cols_hbm, gram_hbm, second_ref, left, acc, pieces, arrive, leave, gram_sem = refs[2 * RING:]
        me_core, me_x, me_y, me_z = (place_ref[i] for i in range(4))

        layout = []
        for kind in range(2):
            by = me_core if kind == 0 else 1 - me_core
            outer_me, inner_me = by * me_y + (1 - by) * me_z, by * me_z + (1 - by) * me_y
            outer_step, inner_step = (width // 8) * (1 - by) + (width // 32) * by, (width // 32) * (1 - by) + (width // 8) * by
            outer = [((outer_me - i) & (RING - 1)) * outer_step + by * half + extra for i in range(RING)]
            layout.append((by, outer, [((inner_me - q) & (RING - 1)) * inner_step for q in range(RING)]))

        def place(t, slot):
            x_hi, c = t >> 1, t & 1
            for kind in range(2):
                by, outer, inner = layout[kind]
                shift_c = (by + c) & 1
                for x_lo in range(2):
                    shift_x = (me_x - x_hi * 2 - x_lo) & (RING - 1)
                    for i in range(RING):
                        for q in range(RING):
                            at = pl.multiple_of(outer[i] + inner[q] + x_lo * (width // 2), half)
                            left[slot, pl.ds(at, half), :] = pieces[kind, i, q, shift_x, shift_c]

        def out_copy(t, slot):
            return pltpu.make_async_copy(left.at[slot, pl.ds(extra, width)], cols_hbm.at[t], leave.at[slot])

        for slot in range(2):
            left[slot, :extra, :] = jnp.zeros((extra, frames), jnp.bfloat16)
        loads = [pltpu.make_async_copy(parts[kind][i], pieces.at[kind, i], arrive.at[kind, i]) for kind in range(2) for i in range(RING)]
        for load in loads:
            load.start()
        for load in loads:
            load.wait()

        def one(t, carry):
            slot = t & 1

            @pl.when(t >= 2)
            def _():
                out_copy(t - 2, slot).wait()

            place(t, slot)
            left[slot, :quarter, :] = rows_ref[t]
            out_copy(t, slot).start()
            strip = width // STRIPS
            for s in range(STRIPS):
                top, end = (extra + s * strip if s else 0), extra + (s + 1) * strip
                part = lax.dot_general(left[slot, top:end, :], left[slot, extra + s * strip:, :], NT, preferred_element_type=jnp.float32)

                @pl.when(t == 0)
                def _():
                    acc[top:end, s * strip:] = part

                @pl.when(t > 0)
                def _():
                    acc[top:end, s * strip:] += part
            return carry

        lax.fori_loop(0, tm_count, one, 0)
        rows = lax.broadcasted_iota(jnp.int32, (NB, width), 0)
        cols = lax.broadcasted_iota(jnp.int32, (NB, width), 1)
        for at in range(0, width, NB):
            cut = pl.ds(extra + at, NB)
            acc[cut, :] = acc[cut, :] * scale + jnp.where(rows + at == cols, noise_ref[...], 0.0)
            pltpu.make_async_copy(acc.at[cut], gram_hbm.at[pl.ds(at, NB)], gram_sem).start()
        second = acc[:quarter, :] * scale
        for i in range(group):
            second_ref[i] = second
        pltpu.make_async_copy(acc.at[pl.ds(extra, width)], gram_hbm, gram_sem).wait()
        out_copy(tm_count - 2, 0).wait()
        out_copy(tm_count - 1, 1).wait()

    anywhere = pl.BlockSpec(memory_space=pl.ANY)
    return pl.pallas_call(
        kernel,
        out_shape=(pltpu.HBM((tm_count, width, frames), jnp.bfloat16), pltpu.HBM((width, width), jnp.float32),
                   jax.ShapeDtypeStruct((group, quarter, width), jnp.float32)),
        in_specs=[SCALARS] + [anywhere] * (2 * RING) + [WHOLE] * 2,
        out_specs=(HBM, HBM, WHOLE),
        scratch_shapes=[pltpu.VMEM((2, width + extra, frames), jnp.bfloat16), pltpu.VMEM((width + extra, width), jnp.float32),
                        pltpu.VMEM((2, RING) + own[0].shape, own[0].dtype), pltpu.SemaphoreType.DMA((2, RING)), pltpu.SemaphoreType.DMA((2,)), pltpu.SemaphoreType.DMA],
        compiler_params=params(40), name="lead_gram")(place, *own, *other, second_rows, noise)


def two(z):
    high = z.astype(jnp.bfloat16)
    return high, (z - high.astype(jnp.float32)).astype(jnp.bfloat16)


def dot3(left, right):
    dot = lambda p, q: lax.dot_general(p, q, NT, preferred_element_type=jnp.float32)
    return dot(left[0], right[0]) + (dot(left[0], right[1]) + dot(left[1], right[0]))


STRIPS = 4


def lower_dot3(left_refs, right_refs, put):
    n = right_refs[0].shape[0]
    step = n // STRIPS
    for s in range(STRIPS):
        rows, k = pl.ds(s * step, step), (s + 1) * step
        put(s * step, step, dot3([r[:, :k] for r in left_refs], [r[rows, :k] for r in right_refs]))


def finish(rows, cols, diag, mine, theirs, inverse, prior, tm_index):
    quarter, cycles, frames = rows[0].shape
    width = cols.shape[1]
    half = width // 2
    plane, group = mine.shape[:2]
    count = quarter * cycles
    scale = 1.0 / (RING * frames)

    def kernel(tm_ref, r0, r1, r2, r3, cols_ref, diag_ref, mine_hbm, theirs_hbm, inv_hbm, prior_hbm, panel_hbm, next_hbm,
               rows_v, acc, gh, gl, prior_v, pieces, inv_v, ih, il, g, sh, sl, sems, row_sems):
        k = pl.program_id(0)
        left = tm_ref[0] % 2 == 0
        fetches = [
            pltpu.make_async_copy(inv_hbm, inv_v, sems.at[0]), pltpu.make_async_copy(mine_hbm, pieces.at[0], sems.at[1]),
            pltpu.make_async_copy(theirs_hbm, pieces.at[1], sems.at[2]), pltpu.make_async_copy(prior_hbm, prior_v, sems.at[3]),
        ]

        @pl.when(k == 0)
        def _():
            for i, r in enumerate((r0, r1, r2, r3)):
                pltpu.make_async_copy(r, rows_v.at[i], row_sems.at[i]).start()
            for f in fetches:
                f.start()

        pltpu.make_async_copy(r0, rows_v.at[k], row_sems.at[k]).wait()
        part = lax.dot_general(rows_v[k].reshape(count, frames), cols_ref[0], NT, preferred_element_type=jnp.float32)

        @pl.when(k == 0)
        def _():
            acc[...] = part.reshape(acc.shape)

        @pl.when(k > 0)
        def _():
            acc[...] += part.reshape(acc.shape)

        @pl.when(k == RING - 1)
        def _():
            for f in fetches:
                f.wait()
            tril = lax.broadcasted_iota(jnp.int32, (width, width), 0) >= lax.broadcasted_iota(jnp.int32, (width, width), 1)
            ih[...], il[...] = two(jnp.where(tril, inv_v[...], 0.0))
            cycle = lax.broadcasted_iota(jnp.int32, (1, cycles, width), 1)
            gram = acc[...] * scale + jnp.where(cycle == 0, diag_ref[...], 0.0)
            gh[...], gl[...] = two(gram.reshape(count, width))

            def put(at, size, value):
                acc[:, :, at:at + size] = value.reshape(quarter, cycles, size)

            lower_dot3([gh, gl], [ih, il], put)
            send_panel = pltpu.make_async_copy(acc, panel_hbm, sems.at[4])
            send_panel.start()

            def place(zy, carry):
                for xc in range(group):
                    at = pl.multiple_of((xc // 2 % 2) * half + zy * (width // 32) + (xc // 4) * 16 + (xc % 2) * 8, 8)
                    u, v = pieces[0, zy, xc], pieces[1, zy, xc]
                    inv_v[pl.ds(at, 8), :half] = jnp.where(left, u, v)
                    inv_v[pl.ds(at, 8), half:] = jnp.where(left, v, u)
                return carry

            lax.fori_loop(0, plane, place, 0)
            g[0], g[1] = two(inv_v[...])

            def put_second(at, size, value):
                sh[:, at:at + size], sl[:, at:at + size] = two(value)

            lower_dot3([g.at[0], g.at[1]], [ih, il], put_second)
            gh[...], gl[...] = two(acc[...].reshape(count, width))
            step = width // STRIPS
            for s in range(STRIPS):
                cut = pl.ds(s * step, step)
                update = dot3([gh[...], gl[...]], [sh[cut, :], sl[cut, :]])
                prior_v[:, :, s * step:(s + 1) * step] = prior_v[:, :, s * step:(s + 1) * step] - update.reshape(quarter, cycles, step)
                part_of = lambda ref: ref.at[:, :, pl.ds(s * step, step)]
                pltpu.make_async_copy(part_of(prior_v), part_of(next_hbm), sems.at[5]).start()
            send_panel.wait()
            pltpu.make_async_copy(prior_v, next_hbm, sems.at[5]).wait()

    out = jax.ShapeDtypeStruct((quarter, cycles, width), jnp.float32)
    square = pltpu.VMEM((width, width), jnp.bfloat16)
    return pl.pallas_call(
        kernel,
        out_shape=(out, out),
        grid_spec=pltpu.PrefetchScalarGridSpec(
            num_scalar_prefetch=1, grid=(RING,),
            in_specs=[HBM] * RING + [pl.BlockSpec((1, width, frames), lambda i, tm: (jnp.bitwise_xor(tm[0], i), 0, 0)),
                      pl.BlockSpec((quarter, 1, width), lambda i, tm: (0, 0, 0))] + [HBM] * 4,
            out_specs=(HBM, HBM),
            scratch_shapes=[pltpu.VMEM((RING, quarter, cycles, frames), jnp.bfloat16), pltpu.VMEM((quarter, cycles, width), jnp.float32)]
            + [pltpu.VMEM((count, width), jnp.bfloat16)] * 2
            + [pltpu.VMEM((quarter, cycles, width), jnp.float32), pltpu.VMEM((2,) + mine.shape, jnp.float32), pltpu.VMEM((width, width), jnp.float32)]
            + [square] * 2 + [pltpu.VMEM((2, width, width), jnp.bfloat16)] + [square] * 2
            + [pltpu.SemaphoreType.DMA((6,)), pltpu.SemaphoreType.DMA((RING,))]),
        compiler_params=params(56), name="finish")(tm_index, *map(in_hbm, rows), cols, diag, in_hbm(mine), in_hbm(theirs), in_hbm(inverse), in_hbm(prior))


def device_id(x, y, z, core):
    return ((x // 2) * 2 + core) * 32 + (x % 2) * 16 + z * 4 + y


DEVICES = [(x, y, z, c) for x in range(RING) for y in range(RING) for z in range(RING) for c in range(2)]


def send(value, step):
    return lax.ppermute(value, AXES, [(device_id(*d), device_id(*step(*d))) for d in DEVICES])


def swap_cores(value):
    return send(value, lambda x, y, z, c: (x, y, z, 1 - c))


def around(value, step):
    return [value] + [send(value, step(d)) for d in range(1, RING)]


def x_ring(d):
    return lambda x, y, z, c: ((x + d) % RING, y, z, c)


def inner_ring(d):
    return lambda x, y, z, c: (x, (y + d * (1 - c)) % RING, (z + d * c) % RING, c)


def outer_ring(d):
    return lambda x, y, z, c: (x, (y + d * c) % RING, (z + d * (1 - c)) % RING, c)


def flip_tm(k):
    return lambda x, y, z, c: (x ^ (k & 2), y, z, c ^ (k & 1))


CHIP_ROWS = [[device_id(x, y, z, c) for x in range(RING) for c in range(2)] for z in range(RING) for y in range(RING)]
PLANES = [[device_id(x, y, z, c) for z in range(RING) for y in range(RING)] for x in range(RING) for c in range(2)]


def shards(telemetry, frame_ids, valid, noise, prior_next):
    slope_index = lax.axis_index("slope")
    tm_index = lax.axis_index("tm")
    tel = telemetry[0]
    row_block, cycles, frames = tel.shape
    width = noise.shape[0]
    tm_count = 4
    quarter = row_block // tm_count
    core_index = tm_index % 2
    place = jnp.stack([core_index, (tm_index // 2) * 2 + slope_index // 16, slope_index % 4, (slope_index // 4) % 4])
    keep = lax.dynamic_slice(valid.reshape(cycles, 4), (0, slope_index // 8), (cycles, 1)).astype(jnp.float32)
    mine, theirs, second_own, hot = pick_first(tel, frame_ids[None, :], valid, jnp.stack([core_index, slope_index // 8]))
    pair = jnp.stack([mine, swap_cores(theirs)])
    by_x = jnp.stack(around(pair, x_ring))
    by_inner = jnp.stack(around(by_x, inner_ring))
    by_inner, hot, second_own = lax.optimization_barrier((by_inner, hot, second_own))
    own = around(by_inner, outer_ring)
    second_rows = lax.all_to_all(second_own.reshape(tm_count, quarter, frames), "tm", 0, 0)
    selected = pick_all(tel, hot, keep, tm_index.reshape(1))
    rows = [selected[0], None, send(selected[2], flip_tm(2)), None]
    other = [swap_cores(piece) for piece in own]
    diag_ids = slope_index * row_block + tm_index * quarter + lax.broadcasted_iota(jnp.int32, (quarter, 1, width), 0)
    diag = jnp.where(diag_ids == lax.broadcasted_iota(jnp.int32, (quarter, 1, width), 2), noise[None, None, :], 0.0)
    selected, own, other, diag = lax.optimization_barrier((selected, own, other, diag))
    first_cols, lead, second_gram = lead_gram(own, other, second_rows, noise[None, :], place)
    near = lax.all_to_all(second_gram, AXES, 0, 0, axis_index_groups=CHIP_ROWS)
    big = chol_step(lead, 0, SPLIT[0])
    near, big, selected = lax.optimization_barrier((near, big, selected))
    rows[3] = send(selected[3], flip_tm(3))
    rows[1] = send(selected[1], flip_tm(1))
    near = lax.dynamic_slice_in_dim(near, core_index * (width // 2), width // 2, axis=2)
    near = jnp.broadcast_to(near[None], (16,) + near.shape)
    mine2 = lax.all_to_all(near, AXES, 0, 0, axis_index_groups=PLANES)
    big = chol_step(big, SPLIT[0], SPLIT[1])
    mine2, big = lax.optimization_barrier((mine2, big))
    theirs2 = swap_cores(mine2)
    big = chol_step(big, SPLIT[0] + SPLIT[1], SPLIT[2])
    panel, next_block = finish(rows, first_cols, diag, mine2, theirs2, big, prior_next[0], tm_index.reshape(1))
    return panel[None], next_block[None]


def solution(mesh):
    return jax.shard_map(
        shards,
        mesh=mesh,
        in_specs=(P("slope", None, None, "tm"), P("tm"), P(), P(), P("slope", "tm", None, None)),
        out_specs=(P("slope", "tm", None, None), P("slope", "tm", None, None)),
        check_vma=False,
    )
```

profile of v0, /device:TPU:0, one launch (start us, length us, event | category | flops | bytes accessed | tf_op | source)
XLA Modules:
  0.0 257.2 jit_solution(7685644398845596094)
XLA Ops:
  0.7 0.7 copy-done.1
  2.1 3.0 %pick_first.1 = (bf16[16,1024]{1,0:T(8,128)(2,1)S(1)}, bf16[16,1024]{1,0:T(8,128)(2,1)S(1)}, bf16[32,1024]{1,0:T(8,128)(2,1)}, bf16[1024,1024]{1,0:T(8,128)(2,1)S(1)}) custom-call(s32[2]{0:T(128)S(1)} %pad_add_fusion.place_ref, bf16[32,96,1024]{2,1,0:T(8,128)(2,1)} %bitcast.28, s32[1,1024]{1,0:T(1,128)S(1)} %bitcast.27, s32[8,48]{1,0:T(8,128)S(1)} %copy-done.1), custom_call_target="tpu_custom_call" | custom-call | tf_op jit(solution)/shard_map/pick_first/pallas_call | solution.py:205
  5.3 1.2 collective-permute-done
  6.5 3.2 %collective-permute-start.2 = (bf16[2,16,1024]{2,1,0:T(8,128)(2,1)S(1)}, bf16[2,16,1024]{2,1,0:T(8,128)(2,1)S(1)}, u32[]{:S(2)}, u32[]{:S(2)}) collective-permute-start(bf16[2,16,1024]{2,1,0:T(8,128)(2,1)S(1)} %get-tuple-element.71), channel_id=1, source_target_pairs={{0,64},{32,96},{4,68},{36,100},{8,72},{40,104},{12,76},{44,108},{1... | collective-permute-start | bytes 196616 | tf_op jit(solution)/shard_map/ppermute | solution.py:460
  10.3 2.6 %collective-permute-start.3 = (bf16[2,16,1024]{2,1,0:T(8,128)(2,1)S(1)}, bf16[2,16,1024]{2,1,0:T(8,128)(2,1)S(1)}, u32[]{:S(2)}, u32[]{:S(2)}) collective-permute-start(bf16[2,16,1024]{2,1,0:T(8,128)(2,1)S(1)} %get-tuple-element.71), channel_id=1, source_target_pairs={{0,80},{32,112},{4,84},{36,116},{8,88},{40,120},{12,92},{44,124},{... | collective-permute-start | bytes 196616 | tf_op jit(solution)/shard_map/ppermute | solution.py:460
  12.9 2.2 collective-permute-done.1
  15.2 3.3 %collective-permute-start.5 = (bf16[4,2,16,1024]{3,2,1,0:T(8,128)(2,1)S(1)}, bf16[4,2,16,1024]{3,2,1,0:T(8,128)(2,1)S(1)}, u32[]{:S(2)}, u32[]{:S(2)}) collective-permute-start(bf16[4,2,16,1024]{3,2,1,0:T(8,128)(2,1)S(1)} %get-tuple-element.69), channel_id=1, source_target_pairs={{0,2},{32,40},{4,6},{36,44},{8,10},{40,32},{12,14},{44,36},{1,3},{... | collective-permute-start | bytes 786440 | tf_op jit(solution)/shard_map/ppermute | solution.py:460
  19.2 2.6 collective-permute-start.6
  21.7 1.4 collective-permute-done.5
  23.2 2.9 %collective-permute-done.4 = bf16[4,2,16,1024]{3,2,1,0:T(8,128)(2,1)S(1)} collective-permute-done((bf16[4,2,16,1024]{3,2,1,0:T(8,128)(2,1)S(1)}, bf16[4,2,16,1024]{3,2,1,0:T(8,128)(2,1)S(1)}, u32[]{:S(2)}, u32[]{:S(2)}) %collective-permute-start.4) | collective-permute-done | bytes 262176 | tf_op jit(solution)/shard_map/ppermute | solution.py:460
  26.5 4.1 %collective-permute-start.9 = (bf16[4,4,2,16,1024]{4,3,2,1,0:T(8,128)(2,1)S(1)}, bf16[4,4,2,16,1024]{4,3,2,1,0:T(8,128)(2,1)}, u32[]{:S(2)}, u32[]{:S(2)}) collective-permute-start(bf16[4,4,2,16,1024]{4,3,2,1,0:T(8,128)(2,1)S(1)} %pad_maximum_fusion.refs_0_), channel_id=1, source_target_pairs={{0,12},{32,35},{4,0},{36,39},{8,4},{40,43},{12,8},{44,47},{1,13},{... | collective-permute-start | bytes 3145736 | tf_op jit(solution)/shard_map/ppermute | solution.py:460
  30.6 1.3 collective-permute-start.7
  31.9 22.2 %collective-permute-done.9.refs_3_ = bf16[4,4,2,16,1024]{4,3,2,1,0:T(8,128)(2,1)} collective-permute-done((bf16[4,4,2,16,1024]{4,3,2,1,0:T(8,128)(2,1)S(1)}, bf16[4,4,2,16,1024]{4,3,2,1,0:T(8,128)(2,1)}, u32[]{:S(2)}, u32[]{:S(2)}) %collective-permute-start.9) | collective-permute-done | bytes 1048608 | tf_op jit(solution)/shard_map/ppermute | solution.py:460
  54.6 3.3 %collective-permute-done.7.refs_1_ = bf16[4,4,2,16,1024]{4,3,2,1,0:T(8,128)(2,1)} collective-permute-done((bf16[4,4,2,16,1024]{4,3,2,1,0:T(8,128)(2,1)S(1)}, bf16[4,4,2,16,1024]{4,3,2,1,0:T(8,128)(2,1)}, u32[]{:S(2)}, u32[]{:S(2)}) %collective-permute-start.7) | collective-permute-done | bytes 1048608 | tf_op jit(solution)/shard_map/ppermute | solution.py:460
  58.2 0.7 compare_select_fusion.diag_ref
  58.9 3.3 %all-to-all-start = ((bf16[4,8,1024]{2,1,0:T(8,128)(2,1)}), bf16[4,8,1024]{2,1,0:T(8,128)(2,1)S(1)}, u32[]{:S(2)}, u32[]{:S(2)}) async-start(bf16[4,8,1024]{2,1,0:T(8,128)(2,1)} %bitcast.18), calls=%async_computation | async-start | bytes 131072 | tf_op jit(solution)/shard_map/all_to_all | solution.py:508
  62.3 12.6 %pick_all.1 = (bf16[8,96,1024]{2,1,0:T(8,128)(2,1)}, bf16[8,96,1024]{2,1,0:T(8,128)(2,1)}, bf16[8,96,1024]{2,1,0:T(8,128)(2,1)}, bf16[8,96,1024]{2,1,0:T(8,128)(2,1)}) custom-call(s32[1]{0:T(128)} %bitcast.tm_ref, bf16[32,96,1024]{2,1,0:T(8,128)(2,1)} %bitcast.29, bf16[1024,1024]{1,0:T(8,128)(2,1)S(1)} %get-tuple-element.39.hot_ref, ...), custom_call_target="tpu_custom_call" | custom-call | tf_op jit(solution)/shard_map/pick_all/pallas_call | solution.py:231
  74.9 17.8 %lead_gram.1 = (bf16[4,1024,1024]{2,1,0:T(8,128)(2,1)}, f32[1024,1024]{1,0:T(8,128)}, f32[8,8,1024]{2,1,0:T(8,128)}) custom-call(s32[4]{0:T(128)S(1)} %pad_add_fusion.1.place_ref, bf16[4,4,2,16,1024]{4,3,2,1,0:T(8,128)(2,1)S(1)} %pad_maximum_fusion.refs_0_, bf16[4,4,2,16,1024]{4,3,2,1,0:T(8,128)(2,1)} %collective-permute-done.7.refs_1_, ...), custom_call_target="tpu_custom_call" | custom-call | tf_op jit(solution)/shard_map/lead_gram/pallas_call | solution.py:324
  92.7 6.4 %all-to-all-start.1 = ((f32[8,8,1024]{2,1,0:T(8,128)}), f32[8,8,1024]{2,1,0:T(8,128)S(1)}, u32[]{:S(2)}, u32[]{:S(2)}) async-start(f32[8,8,1024]{2,1,0:T(8,128)} %get-tuple-element.54), calls=%async_computation.1 | async-start | bytes 524288 | tf_op jit(solution)/shard_map/all_to_all | solution.py:516
  99.1 15.1 %chol_panels.3.src_ref = f32[1024,1024]{1,0:T(8,128)} custom-call(f32[1024,1024]{1,0:T(8,128)} %get-tuple-element.55.src_ref), custom_call_target="tpu_custom_call", output_to_operand_aliasing={{}: (0, {})} | custom-call | tf_op jit(solution)/shard_map/chol_panels/pallas_call | solution.py:170
  114.3 1.6 broadcast_in_dim.35
  115.9 4.4 %all-to-all-start.2 = ((f32[16,8,8,512]{3,2,1,0:T(8,128)}), f32[16,8,8,512]{3,2,1,0:T(8,128)S(1)}, u32[]{:S(2)}, u32[]{:S(2)}) async-start(f32[16,8,8,512]{3,2,1,0:T(8,128)} %broadcast_in_dim.35), calls=%async_computation.2 | async-start | bytes 4194304 | tf_op jit(solution)/shard_map/all_to_all | solution.py:523
  120.3 28.1 %chol_panels.4.src_ref = f32[1024,1024]{1,0:T(8,128)} custom-call(f32[1024,1024]{1,0:T(8,128)} %chol_panels.3.src_ref), custom_call_target="tpu_custom_call", output_to_operand_aliasing={{}: (0, {})} | custom-call | tf_op jit(solution)/shard_map/chol_panels/pallas_call | solution.py:170
  148.4 6.1 %all-to-all-done.2.mine_hbm = f32[16,8,8,512]{3,2,1,0:T(8,128)S(1)} async-done(((f32[16,8,8,512]{3,2,1,0:T(8,128)}), f32[16,8,8,512]{3,2,1,0:T(8,128)S(1)}, u32[]{:S(2)}, u32[]{:S(2)}) %all-to-all-start.2) | async-done | bytes 2097184 | tf_op jit(solution)/shard_map/all_to_all | solution.py:523
  154.4 2.2 collective-permute-start.15
  156.9 1.2 collective-permute-start.16
  158.1 5.8 %chol_panels.5.inv_hbm = f32[1024,1024]{1,0:T(8,128)} custom-call(f32[1024,1024]{1,0:T(8,128)} %chol_panels.4.src_ref), custom_call_target="tpu_custom_call", output_to_operand_aliasing={{}: (0, {})} | custom-call | tf_op jit(solution)/shard_map/chol_panels/pallas_call | solution.py:170
  163.9 29.5 %collective-permute-done.15.r2 = bf16[8,96,1024]{2,1,0:T(8,128)(2,1)S(1)} collective-permute-done((bf16[8,96,1024]{2,1,0:T(8,128)(2,1)}, bf16[8,96,1024]{2,1,0:T(8,128)(2,1)S(1)}, u32[]{:S(2)}, u32[]{:S(2)}) %collective-permute-start.15) | collective-permute-done | bytes 1572896 | tf_op jit(solution)/shard_map/ppermute | solution.py:460
  193.4 32.8 %collective-permute-done.16.r3 = bf16[8,96,1024]{2,1,0:T(8,128)(2,1)S(1)} collective-permute-done((bf16[8,96,1024]{2,1,0:T(8,128)(2,1)}, bf16[8,96,1024]{2,1,0:T(8,128)(2,1)S(1)}, u32[]{:S(2)}, u32[]{:S(2)}) %collective-permute-start.16) | collective-permute-done | bytes 1572896 | tf_op jit(solution)/shard_map/ppermute | solution.py:460
  226.2 1.2 copy-done.8
  227.4 1.4 copy-done.5
  228.7 28.3 %finish.1 = (f32[8,96,1024]{2,1,0:T(8,128)}, f32[8,96,1024]{2,1,0:T(8,128)}) custom-call(s32[1]{0:T(128)} %bitcast.tm_ref, bf16[8,96,1024]{2,1,0:T(8,128)(2,1)} %get-tuple-element.40.r0, bf16[8,96,1024]{2,1,0:T(8,128)(2,1)} %copy-done.7, bf16[8,96,1024]{2,1,0:T(8,128)(2,1)} %copy-done.6, bf16[8,96,1024]{2,1,0:T(8,128)(2,1)} %copy-done.8, ...), custom_call_target="tpu_custom_call" | custom-call | tf_op jit(solution)/shard_map/finish/pallas_call | solution.py:436
  (46 shorter events, 3.6 us)
Async XLA Ops:
  0.7 0.7 copy-start.1
  1.4 0.7 copy-start.3
  5.2 52.8 %copy-start.2 = (s32[8,48]{1,0:T(8,128)S(1)}, s32[8,48]{1,0:T(8,128)}, u32[]{:S(2)}) copy-start(s32[8,48]{1,0:T(8,128)} %valid_ref.1) | copy-start | bytes 4612
  5.2 53.0 %copy-start = (f32[1024]{0:T(1024)S(1)}, f32[1024]{0:T(1024)}, u32[]{:S(2)}) copy-start(f32[1024]{0:T(1024)} %param.8) | copy-start | bytes 12292
  5.2 1.3 collective-permute-start
  6.5 6.5 %collective-permute-start.2 = (bf16[2,16,1024]{2,1,0:T(8,128)(2,1)S(1)}, bf16[2,16,1024]{2,1,0:T(8,128)(2,1)S(1)}, u32[]{:S(2)}, u32[]{:S(2)}) collective-permute-start(bf16[2,16,1024]{2,1,0:T(8,128)(2,1)S(1)} %get-tuple-element.71), channel_id=1, source_target_pairs={{0,64},{32,96},{4,68},{36,100},{8,72},{40,104},{12,76},{44,108},{1... | collective-permute-start | bytes 196616 | tf_op jit(solution)/shard_map/ppermute | solution.py:460
  9.7 5.5 %collective-permute-start.1 = (bf16[2,16,1024]{2,1,0:T(8,128)(2,1)S(1)}, bf16[2,16,1024]{2,1,0:T(8,128)(2,1)S(1)}, u32[]{:S(2)}, u32[]{:S(2)}) collective-permute-start(bf16[2,16,1024]{2,1,0:T(8,128)(2,1)S(1)} %get-tuple-element.71), channel_id=1, source_target_pairs={{0,16},{32,48},{4,20},{36,52},{8,24},{40,56},{12,28},{44,60},{1,17... | collective-permute-start | bytes 196616 | tf_op jit(solution)/shard_map/ppermute | solution.py:460
  10.3 4.9 %collective-permute-start.3 = (bf16[2,16,1024]{2,1,0:T(8,128)(2,1)S(1)}, bf16[2,16,1024]{2,1,0:T(8,128)(2,1)S(1)}, u32[]{:S(2)}, u32[]{:S(2)}) collective-permute-start(bf16[2,16,1024]{2,1,0:T(8,128)(2,1)S(1)} %get-tuple-element.71), channel_id=1, source_target_pairs={{0,80},{32,112},{4,84},{36,116},{8,88},{40,120},{12,92},{44,124},{... | collective-permute-start | bytes 196616 | tf_op jit(solution)/shard_map/ppermute | solution.py:460
  15.2 8.0 %collective-permute-start.5 = (bf16[4,2,16,1024]{3,2,1,0:T(8,128)(2,1)S(1)}, bf16[4,2,16,1024]{3,2,1,0:T(8,128)(2,1)S(1)}, u32[]{:S(2)}, u32[]{:S(2)}) collective-permute-start(bf16[4,2,16,1024]{3,2,1,0:T(8,128)(2,1)S(1)} %get-tuple-element.69), channel_id=1, source_target_pairs={{0,2},{32,40},{4,6},{36,44},{8,10},{40,32},{12,14},{44,36},{1,3},{... | collective-permute-start | bytes 786440 | tf_op jit(solution)/shard_map/ppermute | solution.py:460
  18.5 7.6 %collective-permute-start.4 = (bf16[4,2,16,1024]{3,2,1,0:T(8,128)(2,1)S(1)}, bf16[4,2,16,1024]{3,2,1,0:T(8,128)(2,1)S(1)}, u32[]{:S(2)}, u32[]{:S(2)}) collective-permute-start(bf16[4,2,16,1024]{3,2,1,0:T(8,128)(2,1)S(1)} %get-tuple-element.69), channel_id=1, source_target_pairs={{0,1},{32,36},{4,5},{36,40},{8,9},{40,44},{12,13},{44,32},{1,2},{3... | collective-permute-start | bytes 786440 | tf_op jit(solution)/shard_map/ppermute | solution.py:460
  19.2 7.2 %collective-permute-start.6 = (bf16[4,2,16,1024]{3,2,1,0:T(8,128)(2,1)S(1)}, bf16[4,2,16,1024]{3,2,1,0:T(8,128)(2,1)S(1)}, u32[]{:S(2)}, u32[]{:S(2)}) collective-permute-start(bf16[4,2,16,1024]{3,2,1,0:T(8,128)(2,1)S(1)} %get-tuple-element.69), channel_id=1, source_target_pairs={{0,3},{32,44},{4,7},{36,32},{8,11},{40,36},{12,15},{44,40},{1,0},{... | collective-permute-start | bytes 786440 | tf_op jit(solution)/shard_map/ppermute | solution.py:460
  26.5 27.7 %collective-permute-start.9 = (bf16[4,4,2,16,1024]{4,3,2,1,0:T(8,128)(2,1)S(1)}, bf16[4,4,2,16,1024]{4,3,2,1,0:T(8,128)(2,1)}, u32[]{:S(2)}, u32[]{:S(2)}) collective-permute-start(bf16[4,4,2,16,1024]{4,3,2,1,0:T(8,128)(2,1)S(1)} %pad_maximum_fusion.refs_0_), channel_id=1, source_target_pairs={{0,12},{32,35},{4,0},{36,39},{8,4},{40,43},{12,8},{44,47},{1,13},{... | collective-permute-start | bytes 3145736 | tf_op jit(solution)/shard_map/ppermute | solution.py:460
  30.6 23.6 %collective-permute-start.8 = (bf16[4,4,2,16,1024]{4,3,2,1,0:T(8,128)(2,1)S(1)}, bf16[4,4,2,16,1024]{4,3,2,1,0:T(8,128)(2,1)}, u32[]{:S(2)}, u32[]{:S(2)}) collective-permute-start(bf16[4,4,2,16,1024]{4,3,2,1,0:T(8,128)(2,1)S(1)} %pad_maximum_fusion.refs_0_), channel_id=1, source_target_pairs={{0,8},{32,34},{4,12},{36,38},{8,0},{40,42},{12,4},{44,46},{1,9},{3... | collective-permute-start | bytes 3145736 | tf_op jit(solution)/shard_map/ppermute | solution.py:460
  30.6 27.4 %collective-permute-start.7 = (bf16[4,4,2,16,1024]{4,3,2,1,0:T(8,128)(2,1)S(1)}, bf16[4,4,2,16,1024]{4,3,2,1,0:T(8,128)(2,1)}, u32[]{:S(2)}, u32[]{:S(2)}) collective-permute-start(bf16[4,4,2,16,1024]{4,3,2,1,0:T(8,128)(2,1)S(1)} %pad_maximum_fusion.refs_0_), channel_id=1, source_target_pairs={{0,4},{32,33},{4,8},{36,37},{8,12},{40,41},{12,0},{44,45},{1,5},{3... | collective-permute-start | bytes 3145736 | tf_op jit(solution)/shard_map/ppermute | solution.py:460
  31.9 43.0 %collective-permute-start.10 = (bf16[4,4,2,16,1024]{4,3,2,1,0:T(8,128)(2,1)S(1)}, bf16[4,4,2,16,1024]{4,3,2,1,0:T(8,128)(2,1)}, u32[]{:S(2)}, u32[]{:S(2)}) collective-permute-start(bf16[4,4,2,16,1024]{4,3,2,1,0:T(8,128)(2,1)S(1)} %pad_maximum_fusion.refs_0_), channel_id=1, source_target_pairs={{0,32},{32,0},{4,36},{36,4},{8,40},{40,8},{12,44},{44,12},{1,33},{... | collective-permute-start | bytes 3145736 | tf_op jit(solution)/shard_map/ppermute | solution.py:460
  54.1 20.8 %collective-permute-start.13 = (bf16[4,4,2,16,1024]{4,3,2,1,0:T(8,128)(2,1)}, bf16[4,4,2,16,1024]{4,3,2,1,0:T(8,128)(2,1)}, u32[]{:S(2)}, u32[]{:S(2)}) collective-permute-start(bf16[4,4,2,16,1024]{4,3,2,1,0:T(8,128)(2,1)} %collective-permute-done.9.refs_3_), channel_id=1, source_target_pairs={{0,32},{32,0},{4,36},{36,4},{8,40},{40,8},{12,44},{44,12},{1,33},{... | collective-permute-start | bytes 3145736 | tf_op jit(solution)/shard_map/ppermute | solution.py:460
  54.1 20.8 %collective-permute-start.12 = (bf16[4,4,2,16,1024]{4,3,2,1,0:T(8,128)(2,1)}, bf16[4,4,2,16,1024]{4,3,2,1,0:T(8,128)(2,1)}, u32[]{:S(2)}, u32[]{:S(2)}) collective-permute-start(bf16[4,4,2,16,1024]{4,3,2,1,0:T(8,128)(2,1)} %collective-permute-done.8.refs_2_), channel_id=1, source_target_pairs={{0,32},{32,0},{4,36},{36,4},{8,40},{40,8},{12,44},{44,12},{1,33},{... | collective-permute-start | bytes 3145736 | tf_op jit(solution)/shard_map/ppermute | solution.py:460
  58.0 17.0 %collective-permute-start.11 = (bf16[4,4,2,16,1024]{4,3,2,1,0:T(8,128)(2,1)}, bf16[4,4,2,16,1024]{4,3,2,1,0:T(8,128)(2,1)}, u32[]{:S(2)}, u32[]{:S(2)}) collective-permute-start(bf16[4,4,2,16,1024]{4,3,2,1,0:T(8,128)(2,1)} %collective-permute-done.7.refs_1_), channel_id=1, source_target_pairs={{0,32},{32,0},{4,36},{36,4},{8,40},{40,8},{12,44},{44,12},{1,33},{... | collective-permute-start | bytes 3145736 | tf_op jit(solution)/shard_map/ppermute | solution.py:460
  58.9 16.0 %all-to-all-start = ((bf16[4,8,1024]{2,1,0:T(8,128)(2,1)}), bf16[4,8,1024]{2,1,0:T(8,128)(2,1)S(1)}, u32[]{:S(2)}, u32[]{:S(2)}) async-start(bf16[4,8,1024]{2,1,0:T(8,128)(2,1)} %bitcast.18), calls=%async_computation | async-start | bytes 131072 | tf_op jit(solution)/shard_map/all_to_all | solution.py:508
  92.7 21.5 %all-to-all-start.1 = ((f32[8,8,1024]{2,1,0:T(8,128)}), f32[8,8,1024]{2,1,0:T(8,128)S(1)}, u32[]{:S(2)}, u32[]{:S(2)}) async-start(f32[8,8,1024]{2,1,0:T(8,128)} %get-tuple-element.54), calls=%async_computation.1 | async-start | bytes 524288 | tf_op jit(solution)/shard_map/all_to_all | solution.py:516
  115.9 38.6 %all-to-all-start.2 = ((f32[16,8,8,512]{3,2,1,0:T(8,128)}), f32[16,8,8,512]{3,2,1,0:T(8,128)S(1)}, u32[]{:S(2)}, u32[]{:S(2)}) async-start(f32[16,8,8,512]{3,2,1,0:T(8,128)} %broadcast_in_dim.35), calls=%async_computation.2 | async-start | bytes 4194304 | tf_op jit(solution)/shard_map/all_to_all | solution.py:523
  154.4 9.5 %copy-start.4 = (f32[16,8,8,512]{3,2,1,0:T(8,128)}, f32[16,8,8,512]{3,2,1,0:T(8,128)S(1)}, u32[]{:S(2)}) copy-start(f32[16,8,8,512]{3,2,1,0:T(8,128)S(1)} %all-to-all-done.2.mine_hbm) | copy-start | bytes 6291460
  154.4 71.8 %collective-permute-start.17 = (f32[16,8,8,512]{3,2,1,0:T(8,128)S(1)}, f32[16,8,8,512]{3,2,1,0:T(8,128)S(1)}, u32[]{:S(2)}, u32[]{:S(2)}) collective-permute-start(f32[16,8,8,512]{3,2,1,0:T(8,128)S(1)} %all-to-all-done.2.mine_hbm), channel_id=1, source_target_pairs={{0,32},{32,0},{4,36},{36,4},{8,40},{40,8},{12,44},{44,12},{1,33},{... | collective-permute-start | bytes 6291464 | tf_op jit(solution)/shard_map/ppermute | solution.py:460
  154.4 39.0 %collective-permute-start.15 = (bf16[8,96,1024]{2,1,0:T(8,128)(2,1)}, bf16[8,96,1024]{2,1,0:T(8,128)(2,1)S(1)}, u32[]{:S(2)}, u32[]{:S(2)}) collective-permute-start(bf16[8,96,1024]{2,1,0:T(8,128)(2,1)} %get-tuple-element.42), channel_id=1, source_target_pairs={{0,64},{32,96},{4,68},{36,100},{8,72},{40,104},{12,76},{44,108},{1... | collective-permute-start | bytes 4718600 | tf_op jit(solution)/shard_map/ppermute | solution.py:460
  156.6 36.8 %collective-permute-start.14 = (bf16[8,96,1024]{2,1,0:T(8,128)(2,1)}, bf16[8,96,1024]{2,1,0:T(8,128)(2,1)S(1)}, u32[]{:S(2)}, u32[]{:S(2)}) collective-permute-start(bf16[8,96,1024]{2,1,0:T(8,128)(2,1)} %get-tuple-element.58), channel_id=1, source_target_pairs={{0,32},{32,0},{4,36},{36,4},{8,40},{40,8},{12,44},{44,12},{1,33},{... | collective-permute-start | bytes 4718600 | tf_op jit(solution)/shard_map/ppermute | solution.py:460
  156.9 69.3 %collective-permute-start.16 = (bf16[8,96,1024]{2,1,0:T(8,128)(2,1)}, bf16[8,96,1024]{2,1,0:T(8,128)(2,1)S(1)}, u32[]{:S(2)}, u32[]{:S(2)}) collective-permute-start(bf16[8,96,1024]{2,1,0:T(8,128)(2,1)} %get-tuple-element.59), channel_id=1, source_target_pairs={{0,96},{32,64},{4,100},{36,68},{8,104},{40,72},{12,108},{44,76},{1... | collective-permute-start | bytes 4718600 | tf_op jit(solution)/shard_map/ppermute | solution.py:460
  193.4 34.0 %copy-start.6 = (bf16[8,96,1024]{2,1,0:T(8,128)(2,1)}, bf16[8,96,1024]{2,1,0:T(8,128)(2,1)S(1)}, u32[]{:S(2)}) copy-start(bf16[8,96,1024]{2,1,0:T(8,128)(2,1)S(1)} %collective-permute-done.15.r2) | copy-start | bytes 4718596
  193.4 33.9 %copy-start.7 = (bf16[8,96,1024]{2,1,0:T(8,128)(2,1)}, bf16[8,96,1024]{2,1,0:T(8,128)(2,1)S(1)}, u32[]{:S(2)}) copy-start(bf16[8,96,1024]{2,1,0:T(8,128)(2,1)S(1)} %collective-permute-done.14.r1) | copy-start | bytes 4718596
  226.2 1.2 copy-start.8
  227.4 1.4 copy-start.5
where the time goes:
time: 259 us; the launch traced here: 257 us
  Pallas kernels  111 us (43%)
  waiting for transfers between devices  102 us (39%)
  starting transfers between devices  36.8 us (14%)
  local copies, waits for them, and re-layouts  5.6 us (2%)
    ppermute x18, waiting for transfers between devices, send(): lax.ppermute(value, AXES, [(device_id(*d), device_id(*step(*d))) for d in...  95.8 us
    pallas_call x3, Pallas kernels, chol_step(): pl.pallas_call(kernel, out_shape=pltpu.HBM((n, n), jnp.float32), in_specs...  49.1 us
    pallas_call x1, Pallas kernels, finish(): pl.pallas_call(kernel, out_shape=(out, out), grid_spec=pltpu.PrefetchScal...  28.3 us
    ppermute x18, starting transfers between devices, send(): lax.ppermute(value, AXES, [(device_id(*d), device_id(*step(*d))) for d in...  22.7 us
    pallas_call x1, Pallas kernels, lead_gram(): pl.pallas_call(kernel, out_shape=(pltpu.HBM((tm_count, width, frames), jn...  17.8 us
    pallas_call x1, Pallas kernels, pick_all(): pl.pallas_call(kernel, out_shape=(pltpu.HBM((quarter, cycles, frames), jn...  12.6 us
    all_to_all x1, starting transfers between devices, shards(): near = lax.all_to_all(second_gram, AXES, 0, 0, axis_index_groups=CHIP_ROWS)  6.4 us
    all_to_all x1, waiting for transfers between devices, shards(): mine2 = lax.all_to_all(near, AXES, 0, 0, axis_index_groups=PLANES)  6.08 us
  transfers between devices with their start and end apart: 21, of which 10 were waited for; matrix products, arithmetic and copies ran while one was open for 0% of the time, Pallas kernels for 24%

commit v1 on v0

--- a/solution.py
+++ b/solution.py
@@ -174,18 +174,18 @@
         input_output_aliases={0: 0}, compiler_params=params(24), name="chol_panels")(in_hbm(src))
 
 
-SPLIT = (2, 5, 1)
+SPLIT = (1, 6, 1)
 AXES = ("tm", "slope")
 RING = 4
 SCALARS = pl.BlockSpec(memory_space=pltpu.SMEM)
 HBM = pl.BlockSpec(memory_space=pltpu.HBM)
 
 
-def pick_first(tel, ids, valid, place):
+def pick_first(tel, ids, keep, core):
     rows, _, frames = tel.shape
     half = rows // 2
 
-    def kernel(place_ref, tel_hbm, ids_ref, valid_ref, mine_ref, theirs_ref, second_ref, hot_ref, got, lead, tel_ref, sem):
+    def kernel(core_ref, tel_hbm, ids_ref, keep_ref, mine_ref, theirs_ref, second_ref, hot_ref, got, lead, tel_ref, sem):
         fetch = pltpu.make_async_copy(tel_hbm.at[:, pl.ds(0, 16), :], tel_ref, sem)
         fetch.start()
         hot_ref[...] = jnp.where(lax.broadcasted_iota(jnp.int32, (frames, frames), 0) == ids_ref[...], 1.0, 0.0).astype(jnp.bfloat16)
@@ -193,12 +193,11 @@
         got[...] = tel_ref[...].astype(jnp.float32)
         both = jnp.concatenate([got[:, 0, :], got[:, 1, :]], axis=0).astype(jnp.bfloat16)
         both = jnp.dot(both, hot_ref[...], preferred_element_type=jnp.float32)
-        kept = [valid_ref[0, 4 * c + place_ref[1]].astype(jnp.float32) for c in range(2)]
-        lead[...] = both[:rows] * kept[0]
-        at = pl.multiple_of(place_ref[0] * half, half)
+        lead[...] = both[:rows] * keep_ref[0:1, 0:1]
+        at = pl.multiple_of(core_ref[0] * half, half)
         mine_ref[...] = lead[pl.ds(at, half), :].astype(jnp.bfloat16)
         theirs_ref[...] = lead[pl.ds(pl.multiple_of(half - at, half), half), :].astype(jnp.bfloat16)
-        second_ref[...] = (both[rows:] * kept[1]).astype(jnp.bfloat16)
+        second_ref[...] = (both[rows:] * keep_ref[1:2, 0:1]).astype(jnp.bfloat16)
 
     whole = lambda shape: pl.BlockSpec(shape, lambda i: (0,) * len(shape))
     shapes = ((half, frames), (half, frames), (rows, frames), (frames, frames))
@@ -206,11 +205,11 @@
         kernel,
         grid=(1,),
         out_shape=tuple(jax.ShapeDtypeStruct(s, jnp.bfloat16) for s in shapes),
-        in_specs=[SCALARS, HBM, whole((1, frames)), SCALARS],
+        in_specs=[SCALARS, HBM, whole((1, frames)), whole(keep.shape)],
         out_specs=tuple(whole(s) for s in shapes),
         scratch_shapes=[pltpu.VMEM((rows, 16, frames), jnp.float32), pltpu.VMEM((rows, frames), jnp.float32),
                         pltpu.VMEM((rows, 16, frames), tel.dtype), pltpu.SemaphoreType.DMA],
-        compiler_params=params(), name="pick_first")(place, in_hbm(tel), ids, valid)
+        compiler_params=params(), name="pick_first")(core, in_hbm(tel), ids, keep)
 
 
 def pick_all(tel, hot, keep, tm_index):
@@ -497,9 +496,10 @@
     tm_count = 4
     quarter = row_block // tm_count
     core_index = tm_index % 2
+    core = core_index.reshape(1)
     place = jnp.stack([core_index, (tm_index // 2) * 2 + slope_index // 16, slope_index % 4, (slope_index // 4) % 4])
     keep = lax.dynamic_slice(valid.reshape(cycles, 4), (0, slope_index // 8), (cycles, 1)).astype(jnp.float32)
-    mine, theirs, second_own, hot = pick_first(tel, frame_ids[None, :], valid, jnp.stack([core_index, slope_index // 8]))
+    mine, theirs, second_own, hot = pick_first(tel, frame_ids[None, :], keep, core)
     pair = jnp.stack([mine, swap_cores(theirs)])
     by_x = jnp.stack(around(pair, x_ring))
     by_inner = jnp.stack(around(by_x, inner_ring))
@@ -509,9 +509,7 @@
     selected = pick_all(tel, hot, keep, tm_index.reshape(1))
     rows = [selected[0], None, send(selected[2], flip_tm(2)), None]
     other = [swap_cores(piece) for piece in own]
-    diag_ids = slope_index * row_block + tm_index * quarter + lax.broadcasted_iota(jnp.int32, (quarter, 1, width), 0)
-    diag = jnp.where(diag_ids == lax.broadcasted_iota(jnp.int32, (quarter, 1, width), 2), noise[None, None, :], 0.0)
-    selected, own, other, diag = lax.optimization_barrier((selected, own, other, diag))
+    selected, own, other = lax.optimization_barrier((selected, own, other))
     first_cols, lead, second_gram = lead_gram(own, other, second_rows, noise[None, :], place)
     near = lax.all_to_all(second_gram, AXES, 0, 0, axis_index_groups=CHIP_ROWS)
     big = chol_step(lead, 0, SPLIT[0])
@@ -525,6 +523,8 @@
     mine2, big = lax.optimization_barrier((mine2, big))
     theirs2 = swap_cores(mine2)
     big = chol_step(big, SPLIT[0] + SPLIT[1], SPLIT[2])
+    diag_ids = slope_index * row_block + tm_index * quarter + lax.broadcasted_iota(jnp.int32, (quarter, 1, width), 0)
+    diag = jnp.where(diag_ids == lax.broadcasted_iota(jnp.int32, (quarter, 1, width), 2), noise[None, None, :], 0.0)
     panel, next_block = finish(rows, first_cols, diag, mine2, theirs2, big, prior_next[0], tm_index.reshape(1))
     return panel[None], next_block[None]
 

time: 259 us -> 249 us (0.961)
  waiting for transfers between devices: 102 us -> 95.3 us
    all_to_all x1, waiting for transfers between devices: 6.08 us -> 0.01 us  [shards(): mine2 = lax.all_to_all(near, AXES, 0, 0, axis_index_groups=PLANES)]
    unnamed x18 -> x6, local copies, waits for them, and re-layouts: 3.93 us -> 0.69 us
  transfers between devices with their start and end apart: 21 -> 21, of which waited for: 10 -> 9; matrix products, arithmetic and copies ran while one was open for 0% -> 0% of each run, Pallas kernels for 24% -> 25%
where the time goes in v1:
time: 249 us; the launch traced here: 248 us
  Pallas kernels  110 us (44%)
  waiting for transfers between devices  95.3 us (38%)
  starting transfers between devices  37.1 us (15%)
  local copies, waits for them, and re-layouts  3.06 us (1%)
    ppermute x18, waiting for transfers between devices, send(): lax.ppermute(value, AXES, [(device_id(*d), device_id(*step(*d))) for d in...  95.3 us
    pallas_call x3, Pallas kernels, chol_step(): pl.pallas_call(kernel, out_shape=pltpu.HBM((n, n), jnp.float32), in_specs...  49.1 us
    pallas_call x1, Pallas kernels, finish(): pl.pallas_call(kernel, out_shape=(out, out), grid_spec=pltpu.PrefetchScal...  28.3 us
    ppermute x18, starting transfers between devices, send(): lax.ppermute(value, AXES, [(device_id(*d), device_id(*step(*d))) for d in...  23 us
    pallas_call x1, Pallas kernels, lead_gram(): pl.pallas_call(kernel, out_shape=(pltpu.HBM((tm_count, width, frames), jn...  17.8 us
    pallas_call x1, Pallas kernels, pick_all(): pl.pallas_call(kernel, out_shape=(pltpu.HBM((quarter, cycles, frames), jn...  12.6 us
    all_to_all x1, starting transfers between devices, shards(): near = lax.all_to_all(second_gram, AXES, 0, 0, axis_index_groups=CHIP_ROWS)  6.38 us
  transfers between devices with their start and end apart: 21, of which 9 were waited for; matrix products, arithmetic and copies ran while one was open for 0% of the time, Pallas kernels for 25%

profile of v1, /device:TPU:0, one launch (start us, length us, event | category | flops | bytes accessed | tf_op | source)
XLA Modules:
  0.0 247.6 jit_solution(8127095938322692857)
XLA Ops:
  0.7 0.8 reshape.68
  1.5 0.7 copy-done.1
  2.2 2.4 pick_first.1
  4.7 1.2 collective-permute-done
  5.9 3.2 %collective-permute-start.2 = (bf16[2,16,1024]{2,1,0:T(8,128)(2,1)S(1)}, bf16[2,16,1024]{2,1,0:T(8,128)(2,1)S(1)}, u32[]{:S(2)}, u32[]{:S(2)}) collective-permute-start(bf16[2,16,1024]{2,1,0:T(8,128)(2,1)S(1)} %get-tuple-element.69), channel_id=1, source_target_pairs={{0,64},{32,96},{4,68},{36,100},{8,72},{40,104},{12,76},{44,108},{1... | collective-permute-start | bytes 196616 | tf_op jit(solution)/shard_map/ppermute | solution.py:459
  9.2 0.6 collective-permute-start.1
  9.7 2.6 %collective-permute-start.3 = (bf16[2,16,1024]{2,1,0:T(8,128)(2,1)S(1)}, bf16[2,16,1024]{2,1,0:T(8,128)(2,1)S(1)}, u32[]{:S(2)}, u32[]{:S(2)}) collective-permute-start(bf16[2,16,1024]{2,1,0:T(8,128)(2,1)S(1)} %get-tuple-element.69), channel_id=1, source_target_pairs={{0,80},{32,112},{4,84},{36,116},{8,88},{40,120},{12,92},{44,124},{... | collective-permute-start | bytes 196616 | tf_op jit(solution)/shard_map/ppermute | solution.py:459
  12.4 2.2 collective-permute-done.1
  14.7 3.3 %collective-permute-start.5 = (bf16[4,2,16,1024]{3,2,1,0:T(8,128)(2,1)S(1)}, bf16[4,2,16,1024]{3,2,1,0:T(8,128)(2,1)S(1)}, u32[]{:S(2)}, u32[]{:S(2)}) collective-permute-start(bf16[4,2,16,1024]{3,2,1,0:T(8,128)(2,1)S(1)} %get-tuple-element.67), channel_id=1, source_target_pairs={{0,2},{32,40},{4,6},{36,44},{8,10},{40,32},{12,14},{44,36},{1,3},{... | collective-permute-start | bytes 786440 | tf_op jit(solution)/shard_map/ppermute | solution.py:459
  18.0 0.7 collective-permute-start.4
  18.6 2.6 %collective-permute-start.6 = (bf16[4,2,16,1024]{3,2,1,0:T(8,128)(2,1)S(1)}, bf16[4,2,16,1024]{3,2,1,0:T(8,128)(2,1)S(1)}, u32[]{:S(2)}, u32[]{:S(2)}) collective-permute-start(bf16[4,2,16,1024]{3,2,1,0:T(8,128)(2,1)S(1)} %get-tuple-element.67), channel_id=1, source_target_pairs={{0,3},{32,44},{4,7},{36,32},{8,11},{40,36},{12,15},{44,40},{1,0},{... | collective-permute-start | bytes 786440 | tf_op jit(solution)/shard_map/ppermute | solution.py:459
  21.2 1.4 collective-permute-done.5
  22.6 2.9 %collective-permute-done.4 = bf16[4,2,16,1024]{3,2,1,0:T(8,128)(2,1)S(1)} collective-permute-done((bf16[4,2,16,1024]{3,2,1,0:T(8,128)(2,1)S(1)}, bf16[4,2,16,1024]{3,2,1,0:T(8,128)(2,1)S(1)}, u32[]{:S(2)}, u32[]{:S(2)}) %collective-permute-start.4) | collective-permute-done | bytes 262176 | tf_op jit(solution)/shard_map/ppermute | solution.py:459
  25.9 4.1 %collective-permute-start.9 = (bf16[4,4,2,16,1024]{4,3,2,1,0:T(8,128)(2,1)S(1)}, bf16[4,4,2,16,1024]{4,3,2,1,0:T(8,128)(2,1)}, u32[]{:S(2)}, u32[]{:S(2)}) collective-permute-start(bf16[4,4,2,16,1024]{4,3,2,1,0:T(8,128)(2,1)S(1)} %pad_maximum_fusion.refs_0_), channel_id=1, source_target_pairs={{0,12},{32,35},{4,0},{36,39},{8,4},{40,43},{12,8},{44,47},{1,13},{... | collective-permute-start | bytes 3145736 | tf_op jit(solution)/shard_map/ppermute | solution.py:459
  30.1 1.3 collective-permute-start.7
  31.4 22.2 %collective-permute-done.9.refs_3_ = bf16[4,4,2,16,1024]{4,3,2,1,0:T(8,128)(2,1)} collective-permute-done((bf16[4,4,2,16,1024]{4,3,2,1,0:T(8,128)(2,1)S(1)}, bf16[4,4,2,16,1024]{4,3,2,1,0:T(8,128)(2,1)}, u32[]{:S(2)}, u32[]{:S(2)}) %collective-permute-start.9) | collective-permute-done | bytes 1048608 | tf_op jit(solution)/shard_map/ppermute | solution.py:459
  53.6 0.5 collective-permute-start.12
  54.1 3.3 %collective-permute-done.7.refs_1_ = bf16[4,4,2,16,1024]{4,3,2,1,0:T(8,128)(2,1)} collective-permute-done((bf16[4,4,2,16,1024]{4,3,2,1,0:T(8,128)(2,1)S(1)}, bf16[4,4,2,16,1024]{4,3,2,1,0:T(8,128)(2,1)}, u32[]{:S(2)}, u32[]{:S(2)}) %collective-permute-start.7) | collective-permute-done | bytes 1048608 | tf_op jit(solution)/shard_map/ppermute | solution.py:459
  57.4 3.3 %all-to-all-start = ((bf16[4,8,1024]{2,1,0:T(8,128)(2,1)}), bf16[4,8,1024]{2,1,0:T(8,128)(2,1)S(1)}, u32[]{:S(2)}, u32[]{:S(2)}) async-start(bf16[4,8,1024]{2,1,0:T(8,128)(2,1)} %bitcast.17), calls=%async_computation | async-start | bytes 131072 | tf_op jit(solution)/shard_map/all_to_all | solution.py:508
  60.8 12.6 %pick_all.1 = (bf16[8,96,1024]{2,1,0:T(8,128)(2,1)}, bf16[8,96,1024]{2,1,0:T(8,128)(2,1)}, bf16[8,96,1024]{2,1,0:T(8,128)(2,1)}, bf16[8,96,1024]{2,1,0:T(8,128)(2,1)}) custom-call(s32[1]{0:T(128)} %bitcast.tm_ref, bf16[32,96,1024]{2,1,0:T(8,128)(2,1)} %bitcast.28, bf16[1024,1024]{1,0:T(8,128)(2,1)S(1)} %get-tuple-element.38.hot_ref, ...), custom_call_target="tpu_custom_call" | custom-call | tf_op jit(solution)/shard_map/pick_all/pallas_call | solution.py:230
  73.4 17.8 %lead_gram.1 = (bf16[4,1024,1024]{2,1,0:T(8,128)(2,1)}, f32[1024,1024]{1,0:T(8,128)}, f32[8,8,1024]{2,1,0:T(8,128)}) custom-call(s32[4]{0:T(128)S(1)} %pad_add_fusion.place_ref, bf16[4,4,2,16,1024]{4,3,2,1,0:T(8,128)(2,1)S(1)} %pad_maximum_fusion.refs_0_, bf16[4,4,2,16,1024]{4,3,2,1,0:T(8,128)(2,1)} %collective-permute-done.7.refs_1_, ...), custom_call_target="tpu_custom_call" | custom-call | tf_op jit(solution)/shard_map/lead_gram/pallas_call | solution.py:323
  91.2 6.4 %all-to-all-start.1 = ((f32[8,8,1024]{2,1,0:T(8,128)}), f32[8,8,1024]{2,1,0:T(8,128)S(1)}, u32[]{:S(2)}, u32[]{:S(2)}) async-start(f32[8,8,1024]{2,1,0:T(8,128)} %get-tuple-element.53), calls=%async_computation.1 | async-start | bytes 524288 | tf_op jit(solution)/shard_map/all_to_all | solution.py:514
  97.6 8.9 %chol_panels.3.src_ref = f32[1024,1024]{1,0:T(8,128)} custom-call(f32[1024,1024]{1,0:T(8,128)} %get-tuple-element.54.src_ref), custom_call_target="tpu_custom_call", output_to_operand_aliasing={{}: (0, {})} | custom-call | tf_op jit(solution)/shard_map/chol_panels/pallas_call | solution.py:170
  106.6 1.6 broadcast_in_dim.35
  108.1 4.4 %all-to-all-start.2 = ((f32[16,8,8,512]{3,2,1,0:T(8,128)}), f32[16,8,8,512]{3,2,1,0:T(8,128)S(1)}, u32[]{:S(2)}, u32[]{:S(2)}) async-start(f32[16,8,8,512]{3,2,1,0:T(8,128)} %broadcast_in_dim.35), calls=%async_computation.2 | async-start | bytes 4194304 | tf_op jit(solution)/shard_map/all_to_all | solution.py:521
  112.6 34.3 %chol_panels.4.src_ref = f32[1024,1024]{1,0:T(8,128)} custom-call(f32[1024,1024]{1,0:T(8,128)} %chol_panels.3.src_ref), custom_call_target="tpu_custom_call", output_to_operand_aliasing={{}: (0, {})} | custom-call | tf_op jit(solution)/shard_map/chol_panels/pallas_call | solution.py:170
  147.2 3.4 %collective-permute-start.15 = (bf16[8,96,1024]{2,1,0:T(8,128)(2,1)}, bf16[8,96,1024]{2,1,0:T(8,128)(2,1)}, u32[]{:S(2)}, u32[]{:S(2)}) collective-permute-start(bf16[8,96,1024]{2,1,0:T(8,128)(2,1)} %get-tuple-element.41), channel_id=1, source_target_pairs={{0,64},{32,96},{4,68},{36,100},{8,72},{40,104},{12,76},{44,108},{1... | collective-permute-start | bytes 4718600 | tf_op jit(solution)/shard_map/ppermute | solution.py:459
  150.8 0.7 compare_select_fusion.diag_ref
  151.5 5.9 %chol_panels.5.inv_hbm = f32[1024,1024]{1,0:T(8,128)} custom-call(f32[1024,1024]{1,0:T(8,128)} %chol_panels.4.src_ref), custom_call_target="tpu_custom_call", output_to_operand_aliasing={{}: (0, {})} | custom-call | tf_op jit(solution)/shard_map/chol_panels/pallas_call | solution.py:170
  157.4 28.9 %collective-permute-done.15.r2 = bf16[8,96,1024]{2,1,0:T(8,128)(2,1)} collective-permute-done((bf16[8,96,1024]{2,1,0:T(8,128)(2,1)}, bf16[8,96,1024]{2,1,0:T(8,128)(2,1)}, u32[]{:S(2)}, u32[]{:S(2)}) %collective-permute-start.15) | collective-permute-done | bytes 1572896 | tf_op jit(solution)/shard_map/ppermute | solution.py:459
  186.3 32.9 %collective-permute-done.16.r3 = bf16[8,96,1024]{2,1,0:T(8,128)(2,1)} collective-permute-done((bf16[8,96,1024]{2,1,0:T(8,128)(2,1)}, bf16[8,96,1024]{2,1,0:T(8,128)(2,1)}, u32[]{:S(2)}, u32[]{:S(2)}) %collective-permute-start.16) | collective-permute-done | bytes 1572896 | tf_op jit(solution)/shard_map/ppermute | solution.py:459
  219.2 28.3 %finish.1 = (f32[8,96,1024]{2,1,0:T(8,128)}, f32[8,96,1024]{2,1,0:T(8,128)}) custom-call(s32[1]{0:T(128)} %bitcast.tm_ref, bf16[8,96,1024]{2,1,0:T(8,128)(2,1)} %get-tuple-element.39.r0, bf16[8,96,1024]{2,1,0:T(8,128)(2,1)} %collective-permute-done.14.r1, bf16[8,96,1024]{2,1,0:T(8,128)(2,1)} %collective-permute-done.15.r2, ...), custom_call_target="tpu_custom_call" | custom-call | tf_op jit(solution)/shard_map/finish/pallas_call | solution.py:435
  (33 shorter events, 1.3 us)
Async XLA Ops:
  1.5 0.7 copy-start.1
  4.6 1.3 collective-permute-start
  5.9 6.5 %collective-permute-start.2 = (bf16[2,16,1024]{2,1,0:T(8,128)(2,1)S(1)}, bf16[2,16,1024]{2,1,0:T(8,128)(2,1)S(1)}, u32[]{:S(2)}, u32[]{:S(2)}) collective-permute-start(bf16[2,16,1024]{2,1,0:T(8,128)(2,1)S(1)} %get-tuple-element.69), channel_id=1, source_target_pairs={{0,64},{32,96},{4,68},{36,100},{8,72},{40,104},{12,76},{44,108},{1... | collective-permute-start | bytes 196616 | tf_op jit(solution)/shard_map/ppermute | solution.py:459
  9.2 5.5 %collective-permute-start.1 = (bf16[2,16,1024]{2,1,0:T(8,128)(2,1)S(1)}, bf16[2,16,1024]{2,1,0:T(8,128)(2,1)S(1)}, u32[]{:S(2)}, u32[]{:S(2)}) collective-permute-start(bf16[2,16,1024]{2,1,0:T(8,128)(2,1)S(1)} %get-tuple-element.69), channel_id=1, source_target_pairs={{0,16},{32,48},{4,20},{36,52},{8,24},{40,56},{12,28},{44,60},{1,17... | collective-permute-start | bytes 196616 | tf_op jit(solution)/shard_map/ppermute | solution.py:459
  9.7 4.9 %collective-permute-start.3 = (bf16[2,16,1024]{2,1,0:T(8,128)(2,1)S(1)}, bf16[2,16,1024]{2,1,0:T(8,128)(2,1)S(1)}, u32[]{:S(2)}, u32[]{:S(2)}) collective-permute-start(bf16[2,16,1024]{2,1,0:T(8,128)(2,1)S(1)} %get-tuple-element.69), channel_id=1, source_target_pairs={{0,80},{32,112},{4,84},{36,116},{8,88},{40,120},{12,92},{44,124},{... | collective-permute-start | bytes 196616 | tf_op jit(solution)/shard_map/ppermute | solution.py:459
  14.7 8.0 %collective-permute-start.5 = (bf16[4,2,16,1024]{3,2,1,0:T(8,128)(2,1)S(1)}, bf16[4,2,16,1024]{3,2,1,0:T(8,128)(2,1)S(1)}, u32[]{:S(2)}, u32[]{:S(2)}) collective-permute-start(bf16[4,2,16,1024]{3,2,1,0:T(8,128)(2,1)S(1)} %get-tuple-element.67), channel_id=1, source_target_pairs={{0,2},{32,40},{4,6},{36,44},{8,10},{40,32},{12,14},{44,36},{1,3},{... | collective-permute-start | bytes 786440 | tf_op jit(solution)/shard_map/ppermute | solution.py:459
  18.0 7.6 %collective-permute-start.4 = (bf16[4,2,16,1024]{3,2,1,0:T(8,128)(2,1)S(1)}, bf16[4,2,16,1024]{3,2,1,0:T(8,128)(2,1)S(1)}, u32[]{:S(2)}, u32[]{:S(2)}) collective-permute-start(bf16[4,2,16,1024]{3,2,1,0:T(8,128)(2,1)S(1)} %get-tuple-element.67), channel_id=1, source_target_pairs={{0,1},{32,36},{4,5},{36,40},{8,9},{40,44},{12,13},{44,32},{1,2},{3... | collective-permute-start | bytes 786440 | tf_op jit(solution)/shard_map/ppermute | solution.py:459
  18.6 7.2 %collective-permute-start.6 = (bf16[4,2,16,1024]{3,2,1,0:T(8,128)(2,1)S(1)}, bf16[4,2,16,1024]{3,2,1,0:T(8,128)(2,1)S(1)}, u32[]{:S(2)}, u32[]{:S(2)}) collective-permute-start(bf16[4,2,16,1024]{3,2,1,0:T(8,128)(2,1)S(1)} %get-tuple-element.67), channel_id=1, source_target_pairs={{0,3},{32,44},{4,7},{36,32},{8,11},{40,36},{12,15},{44,40},{1,0},{... | collective-permute-start | bytes 786440 | tf_op jit(solution)/shard_map/ppermute | solution.py:459
  25.9 27.7 %collective-permute-start.9 = (bf16[4,4,2,16,1024]{4,3,2,1,0:T(8,128)(2,1)S(1)}, bf16[4,4,2,16,1024]{4,3,2,1,0:T(8,128)(2,1)}, u32[]{:S(2)}, u32[]{:S(2)}) collective-permute-start(bf16[4,4,2,16,1024]{4,3,2,1,0:T(8,128)(2,1)S(1)} %pad_maximum_fusion.refs_0_), channel_id=1, source_target_pairs={{0,12},{32,35},{4,0},{36,39},{8,4},{40,43},{12,8},{44,47},{1,13},{... | collective-permute-start | bytes 3145736 | tf_op jit(solution)/shard_map/ppermute | solution.py:459
  30.0 23.6 %collective-permute-start.8 = (bf16[4,4,2,16,1024]{4,3,2,1,0:T(8,128)(2,1)S(1)}, bf16[4,4,2,16,1024]{4,3,2,1,0:T(8,128)(2,1)}, u32[]{:S(2)}, u32[]{:S(2)}) collective-permute-start(bf16[4,4,2,16,1024]{4,3,2,1,0:T(8,128)(2,1)S(1)} %pad_maximum_fusion.refs_0_), channel_id=1, source_target_pairs={{0,8},{32,34},{4,12},{36,38},{8,0},{40,42},{12,4},{44,46},{1,9},{3... | collective-permute-start | bytes 3145736 | tf_op jit(solution)/shard_map/ppermute | solution.py:459
  30.1 27.4 %collective-permute-start.7 = (bf16[4,4,2,16,1024]{4,3,2,1,0:T(8,128)(2,1)S(1)}, bf16[4,4,2,16,1024]{4,3,2,1,0:T(8,128)(2,1)}, u32[]{:S(2)}, u32[]{:S(2)}) collective-permute-start(bf16[4,4,2,16,1024]{4,3,2,1,0:T(8,128)(2,1)S(1)} %pad_maximum_fusion.refs_0_), channel_id=1, source_target_pairs={{0,4},{32,33},{4,8},{36,37},{8,12},{40,41},{12,0},{44,45},{1,5},{3... | collective-permute-start | bytes 3145736 | tf_op jit(solution)/shard_map/ppermute | solution.py:459
  31.4 42.0 %collective-permute-start.10 = (bf16[4,4,2,16,1024]{4,3,2,1,0:T(8,128)(2,1)S(1)}, bf16[4,4,2,16,1024]{4,3,2,1,0:T(8,128)(2,1)}, u32[]{:S(2)}, u32[]{:S(2)}) collective-permute-start(bf16[4,4,2,16,1024]{4,3,2,1,0:T(8,128)(2,1)S(1)} %pad_maximum_fusion.refs_0_), channel_id=1, source_target_pairs={{0,32},{32,0},{4,36},{36,4},{8,40},{40,8},{12,44},{44,12},{1,33},{... | collective-permute-start | bytes 3145736 | tf_op jit(solution)/shard_map/ppermute | solution.py:459
  53.6 19.8 %collective-permute-start.13 = (bf16[4,4,2,16,1024]{4,3,2,1,0:T(8,128)(2,1)}, bf16[4,4,2,16,1024]{4,3,2,1,0:T(8,128)(2,1)}, u32[]{:S(2)}, u32[]{:S(2)}) collective-permute-start(bf16[4,4,2,16,1024]{4,3,2,1,0:T(8,128)(2,1)} %collective-permute-done.9.refs_3_), channel_id=1, source_target_pairs={{0,32},{32,0},{4,36},{36,4},{8,40},{40,8},{12,44},{44,12},{1,33},{... | collective-permute-start | bytes 3145736 | tf_op jit(solution)/shard_map/ppermute | solution.py:459
  53.6 19.8 %collective-permute-start.12 = (bf16[4,4,2,16,1024]{4,3,2,1,0:T(8,128)(2,1)}, bf16[4,4,2,16,1024]{4,3,2,1,0:T(8,128)(2,1)}, u32[]{:S(2)}, u32[]{:S(2)}) collective-permute-start(bf16[4,4,2,16,1024]{4,3,2,1,0:T(8,128)(2,1)} %collective-permute-done.8.refs_2_), channel_id=1, source_target_pairs={{0,32},{32,0},{4,36},{36,4},{8,40},{40,8},{12,44},{44,12},{1,33},{... | collective-permute-start | bytes 3145736 | tf_op jit(solution)/shard_map/ppermute | solution.py:459
  57.4 16.0 %collective-permute-start.11 = (bf16[4,4,2,16,1024]{4,3,2,1,0:T(8,128)(2,1)}, bf16[4,4,2,16,1024]{4,3,2,1,0:T(8,128)(2,1)}, u32[]{:S(2)}, u32[]{:S(2)}) collective-permute-start(bf16[4,4,2,16,1024]{4,3,2,1,0:T(8,128)(2,1)} %collective-permute-done.7.refs_1_), channel_id=1, source_target_pairs={{0,32},{32,0},{4,36},{36,4},{8,40},{40,8},{12,44},{44,12},{1,33},{... | collective-permute-start | bytes 3145736 | tf_op jit(solution)/shard_map/ppermute | solution.py:459
  57.4 16.0 %all-to-all-start = ((bf16[4,8,1024]{2,1,0:T(8,128)(2,1)}), bf16[4,8,1024]{2,1,0:T(8,128)(2,1)S(1)}, u32[]{:S(2)}, u32[]{:S(2)}) async-start(bf16[4,8,1024]{2,1,0:T(8,128)(2,1)} %bitcast.17), calls=%async_computation | async-start | bytes 131072 | tf_op jit(solution)/shard_map/all_to_all | solution.py:508
  60.8 12.6 %copy-start = (f32[1024]{0:T(1024)S(1)}, f32[1024]{0:T(1024)}, u32[]{:S(2)}) copy-start(f32[1024]{0:T(1024)} %param.8) | copy-start | bytes 12292
  91.2 15.3 %all-to-all-start.1 = ((f32[8,8,1024]{2,1,0:T(8,128)}), f32[8,8,1024]{2,1,0:T(8,128)S(1)}, u32[]{:S(2)}, u32[]{:S(2)}) async-start(f32[8,8,1024]{2,1,0:T(8,128)} %get-tuple-element.53), calls=%async_computation.1 | async-start | bytes 524288 | tf_op jit(solution)/shard_map/all_to_all | solution.py:514
  108.1 38.7 %all-to-all-start.2 = ((f32[16,8,8,512]{3,2,1,0:T(8,128)}), f32[16,8,8,512]{3,2,1,0:T(8,128)S(1)}, u32[]{:S(2)}, u32[]{:S(2)}) async-start(f32[16,8,8,512]{3,2,1,0:T(8,128)} %broadcast_in_dim.35), calls=%async_computation.2 | async-start | bytes 4194304 | tf_op jit(solution)/shard_map/all_to_all | solution.py:521
  146.9 10.5 %copy-start.2 = (f32[16,8,8,512]{3,2,1,0:T(8,128)}, f32[16,8,8,512]{3,2,1,0:T(8,128)S(1)}, u32[]{:S(2)}) copy-start(f32[16,8,8,512]{3,2,1,0:T(8,128)S(1)} %all-to-all-done.2.mine_hbm) | copy-start | bytes 6291460
  146.9 72.3 %collective-permute-start.17 = (f32[16,8,8,512]{3,2,1,0:T(8,128)S(1)}, f32[16,8,8,512]{3,2,1,0:T(8,128)}, u32[]{:S(2)}, u32[]{:S(2)}) collective-permute-start(f32[16,8,8,512]{3,2,1,0:T(8,128)S(1)} %all-to-all-done.2.mine_hbm), channel_id=1, source_target_pairs={{0,32},{32,0},{4,36},{36,4},{8,40},{40,8},{12,44},{44,12},{1,33},{... | collective-permute-start | bytes 6291464 | tf_op jit(solution)/shard_map/ppermute | solution.py:459
  147.2 39.1 %collective-permute-start.15 = (bf16[8,96,1024]{2,1,0:T(8,128)(2,1)}, bf16[8,96,1024]{2,1,0:T(8,128)(2,1)}, u32[]{:S(2)}, u32[]{:S(2)}) collective-permute-start(bf16[8,96,1024]{2,1,0:T(8,128)(2,1)} %get-tuple-element.41), channel_id=1, source_target_pairs={{0,64},{32,96},{4,68},{36,100},{8,72},{40,104},{12,76},{44,108},{1... | collective-permute-start | bytes 4718600 | tf_op jit(solution)/shard_map/ppermute | solution.py:459
  150.6 35.7 %collective-permute-start.14 = (bf16[8,96,1024]{2,1,0:T(8,128)(2,1)}, bf16[8,96,1024]{2,1,0:T(8,128)(2,1)}, u32[]{:S(2)}, u32[]{:S(2)}) collective-permute-start(bf16[8,96,1024]{2,1,0:T(8,128)(2,1)} %get-tuple-element.57), channel_id=1, source_target_pairs={{0,32},{32,0},{4,36},{36,4},{8,40},{40,8},{12,44},{44,12},{1,33},{... | collective-permute-start | bytes 4718600 | tf_op jit(solution)/shard_map/ppermute | solution.py:459
  150.7 68.4 %collective-permute-start.16 = (bf16[8,96,1024]{2,1,0:T(8,128)(2,1)}, bf16[8,96,1024]{2,1,0:T(8,128)(2,1)}, u32[]{:S(2)}, u32[]{:S(2)}) collective-permute-start(bf16[8,96,1024]{2,1,0:T(8,128)(2,1)} %get-tuple-element.58), channel_id=1, source_target_pairs={{0,96},{32,64},{4,100},{36,68},{8,104},{40,72},{12,108},{44,76},{1... | collective-permute-start | bytes 4718600 | tf_op jit(solution)/shard_map/ppermute | solution.py:459
